TPU v7x, 32 devices: a whole 2x2x4 slice. The times are simulated.
32 devices in a mesh: dp: 8 (over y, x, core), tensor: 4 (over z).
Axes of the slice: x: 2, y: 2, z: 4, core: 2. Of those that a mesh axis runs over, the one named last changes fastest.
Arguments:
- tokens: bfloat16 [1024, 8192], P('dp'), may hold values from -6 to 6
- target: bfloat16 [1024, 8192], P('dp'), may hold values from -6 to 6
- weight_in: bfloat16 [8192, 16384], P('dp', 'tensor'), may hold values from -0.125 to 0.125
- weight_out: bfloat16 [16384, 8192], P('tensor', 'dp'), may hold values from -0.09375 to 0.09375
- pattern: int32 [64, 128], replicated, may hold values from 0 to 1, as said below
Outputs:
- output: bfloat16 [1024, 8192], P('dp', 'tensor')
- hidden_target: bfloat16 [1024, 16384], P('dp', 'tensor')
Inputs may be any that keep to these rules, and one draw needn't show every extreme that they name: `pattern`: every entry is 0 or 1. A tile is the 8 row blocks of one index of dp with the 32 hidden blocks of one index of tensor; no tile holds more than 64 ones, and in every draw all tiles of one index of tensor hold exactly 64.
All inputs are finite; a program needn't handle non-finite values.
Results may differ from a plain program's by a relative error of at most 0.013.
Values may be sent and summed in bfloat16 or wider, within the bound.
A program may use at most 128 MiB of HBM per device.

v0:
```python
import jax
import jax.numpy as jnp
from jax import lax
from jax.sharding import PartitionSpec as P

BLK = 128


def slot_layout(pattern, column_start, blocks_down, blocks_across, peer_count, capacity):
    strip = lax.dynamic_slice_in_dim(pattern, column_start, blocks_across, 1)
    tile_size = blocks_down * blocks_across
    flat_mask = strip.reshape(peer_count, tile_size)
    position = jnp.cumsum(flat_mask, axis=1) - 1
    wanted = jnp.arange(capacity, dtype=jnp.int32)
    chosen = (
        (flat_mask[:, None, :] == 1) & (position[:, None, :] == wanted[None, :, None])
    ).astype(jnp.int32)
    within = jnp.sum(chosen * jnp.arange(tile_size, dtype=jnp.int32)[None, None, :], axis=2)
    return (chosen, within)


def one_hot_rows(index, count, dtype):
    return (index[:, None] == jnp.arange(count, dtype=jnp.int32)[None, :]).astype(dtype)


def spread_blocks(running, sources, weights, row_index, hidden_index, formula):
    row_hot = one_hot_rows(row_index, sources.shape[1], sources.dtype)
    picked = jnp.einsum("trb,sr->tsb", sources, row_hot, preferred_element_type=jnp.float32).astype(
        sources.dtype
    )
    product = jnp.einsum(formula, picked, weights, preferred_element_type=jnp.float32)
    hidden_hot = one_hot_rows(hidden_index, running.shape[1], jnp.float32)
    placed = jnp.einsum(
        "tsc,sj->tjc",
        product,
        hidden_hot,
        precision=lax.Precision.HIGHEST,
        preferred_element_type=jnp.float32,
    )
    return running + placed


def sweep_slots(running, sources, weights, row_index, hidden_index, formula, slot_step):
    slot_count = weights.shape[0]

    def advance(turn_index, carry):
        offset = turn_index * slot_step
        return spread_blocks(
            carry,
            sources,
            lax.dynamic_slice_in_dim(weights, offset, slot_step),
            lax.dynamic_slice_in_dim(row_index, offset, slot_step),
            lax.dynamic_slice_in_dim(hidden_index, offset, slot_step),
            formula,
        )

    return lax.fori_loop(0, slot_count // slot_step, advance, running)


def shards(tokens, target, weight_in, weight_out, pattern):
    peer_count = lax.axis_size("dp")
    data_rank = lax.axis_index("dp")
    tensor_rank = lax.axis_index("tensor")
    blocks_down = weight_in.shape[0] // BLK
    blocks_across = weight_in.shape[1] // BLK
    tile_size = blocks_down * blocks_across
    capacity = max(2, tile_size // 4)
    tok_rows = tokens.shape[0]
    all_rows = tokens.shape[1] // BLK
    chosen, within = slot_layout(
        pattern, tensor_rank * blocks_across, blocks_down, blocks_across, peer_count, capacity
    )
    own_pick = lax.dynamic_index_in_dim(chosen, data_rank, 0, keepdims=False).astype(jnp.bfloat16)
    in_tile = (
        weight_in.reshape(blocks_down, BLK, blocks_across, BLK)
        .transpose(0, 2, 1, 3)
        .reshape(tile_size, BLK, BLK)
    )
    out_tile = (
        weight_out.reshape(blocks_across, BLK, blocks_down, BLK)
        .transpose(2, 0, 1, 3)
        .reshape(tile_size, BLK, BLK)
    )
    packed_in = jnp.einsum(
        "cb,bxy->cxy", own_pick, in_tile, preferred_element_type=jnp.float32
    ).astype(jnp.bfloat16)
    packed_out = jnp.einsum(
        "cb,bxy->cxy", own_pick, out_tile, preferred_element_type=jnp.float32
    ).astype(jnp.bfloat16)
    local_row = within // blocks_across
    slot_hidden = (within % blocks_across).reshape(-1)
    slot_row = (local_row + jnp.arange(peer_count, dtype=jnp.int32)[:, None] * blocks_down).reshape(
        -1
    )
    group_peers = 1
    while group_peers * 2 * capacity <= 64 and peer_count % (group_peers * 2) == 0:
        group_peers = group_peers * 2
    slot_step = group_peers * capacity
    group_count = peer_count // group_peers
    token_blocks = tokens.reshape(tok_rows, all_rows, BLK)
    empty = jnp.zeros((tok_rows, blocks_across, BLK), jnp.float32)
    gathered_in, gathered_out = (
        lax.all_gather(packed_in, "dp", axis=0, tiled=True),
        lax.all_gather(packed_out, "dp", axis=0, tiled=True),
    )
    hidden = sweep_slots(
        empty, token_blocks, gathered_in, slot_row, slot_hidden, "tsb,sbc->tsc", slot_step
    )
    active = jnp.tanh(hidden).astype(jnp.bfloat16)
    place_count = group_peers * blocks_down
    peer_offset = jnp.arange(group_peers, dtype=jnp.int32)[:, None] * blocks_down

    def emit_rows(group_args):
        weights, hidden_index, row_index = group_args
        hidden_hot = one_hot_rows(hidden_index, blocks_across, jnp.bfloat16)
        picked = jnp.einsum(
            "tjh,sj->tsh", active, hidden_hot, preferred_element_type=jnp.float32
        ).astype(jnp.bfloat16)
        product = jnp.einsum("tsh,shd->tsd", picked, weights, preferred_element_type=jnp.float32)
        place_index = (row_index + peer_offset).reshape(-1)
        place_hot = one_hot_rows(place_index, place_count, jnp.float32)
        return jnp.einsum(
            "tsd,sq->tqd",
            product,
            place_hot,
            precision=lax.Precision.HIGHEST,
            preferred_element_type=jnp.float32,
        )

    pieces = lax.map(
        emit_rows,
        (
            gathered_out.reshape(group_count, slot_step, BLK, BLK),
            slot_hidden.reshape(group_count, slot_step),
            local_row.reshape(group_count, group_peers, capacity),
        ),
    )
    partial_value = pieces.transpose(1, 0, 2, 3).reshape(tok_rows, -1).astype(jnp.bfloat16)
    summed = lax.psum(partial_value, "tensor").astype(jnp.float32)
    whole_out = summed.astype(jnp.bfloat16)
    share_width = whole_out.shape[1] // lax.axis_size("tensor")
    output = lax.dynamic_slice_in_dim(whole_out, tensor_rank * share_width, share_width, 1)
    stacked = jnp.concatenate([whole_out, target], axis=0).reshape(2 * tok_rows, all_rows, BLK)
    zero_image = jnp.zeros((2 * tok_rows, blocks_across, BLK), jnp.float32)
    image = sweep_slots(
        zero_image, stacked, gathered_out, slot_row, slot_hidden, "tsd,shd->tsh", slot_step
    )
    feedback = jnp.tanh(image)
    hidden_target = active.astype(jnp.float32) + feedback[tok_rows:] - feedback[:tok_rows]
    return (output, hidden_target.reshape(tok_rows, -1).astype(jnp.bfloat16))


def solution(mesh):
    in_specs = (P("dp", None), P("dp", None), P("dp", "tensor"), P("tensor", "dp"), P())
    out_specs = (P("dp", "tensor"), P("dp", "tensor"))
    return jax.shard_map(shards, mesh=mesh, in_specs=in_specs, out_specs=out_specs, check_vma=False)
```

profile of v0, /device:TPU:0, one launch (start us, length us, event | category | flops | bytes accessed | tf_op | source)
XLA Modules:
  0.0 778.2 jit_solution(2342957863478818360)
XLA Ops:
  9.2 9.4 %copy.32 = bf16[128,8,32,128]{3,2,1,0:T(8,128)(2,1)} copy(bf16[128,8,32,128]{3,1,2,0:T(8,128)(2,1)} %bitcast.174) | data formatting | bytes 16777216
  26.6 9.2 %copy.16 = bf16[8,32,128,128]{3,1,0,2:T(8,128)(2,1)} copy(bf16[8,32,128,128]{3,1,2,0:T(8,128)(2,1)} %bitcast_bitcast_fusion) | data formatting | bytes 16777216 | tf_op jit(solution)/shard_map/transpose | solution.py:76
  42.8 8.8 %copy.31 = bf16[512,8,8,128]{3,2,1,0:T(8,128)(2,1)} copy(bf16[512,8,8,128]{3,1,2,0:T(8,128)(2,1)} %bitcast.175) | data formatting | bytes 16777216
  60.2 16.5 %copy.15 = bf16[8,32,128,128]{3,1,0,2:T(8,128)(2,1)} copy(bf16[8,32,128,128]{3,0,2,1:T(8,128)(2,1)} %bitcast_bitcast_fusion.1) | data formatting | bytes 16777216 | tf_op jit(solution)/shard_map/transpose | solution.py:81
  87.2 47.7 %all-gather.5.cloned.1.call-done = bf16[512,128,128]{2,0,1:T(8,128)(2,1)} async-done(((bf16[64,128,128]{2,0,1:T(8,128)(2,1)}), bf16[512,128,128]{2,0,1:T(8,128)(2,1)}) %all-gather.5.cloned.1.call-update) | async-done | bytes 16777232 | tf_op jit(solution)/shard_map/all_gather | solution.py:103
  134.9 148.5 %while.39 = (s32[]{:T(128)}, f32[128,32,128]{2,1,0:T(8,128)S(1)}, s32[512]{0:T(512)S(1)}, bf16[512,128,128]{2,0,1:T(8,128)(2,1)}, s32[512]{0:T(512)S(1)}, /*inde...) while((s32[]{:T(128)}, f32[128,32,128]{2,1,0:T(8,128)S(1)}, ...), condition=%wide.region_4.5_spmd.clone, body=%wide.region_3.4_spmd.clone.sunk | while | flops 806361088 | bytes 41944780 | solution.py:57
  283.7 137.5 %while.38 = (s32[]{:T(128)}, bf16[8,128,8,128]{3,2,1,0:T(8,128)(2,1)}, s32[8,1,64]{2,1,0:T(1,128)S(1)}, bf16[8,64,128,128]{3,1,0,2:T(8,128)(2,1)}, s32[8,64]{1,0...) while((s32[]{:T(128)}, bf16[8,128,8,128]{3,2,1,0:T(8,128)(2,1)}, s32[8,1,64]{2,1,0:T(1,128)S(1)}, ...), condition=%wide.region_6.7_spmd, body=%wide.region_5.6_spmd.sunk | while | flops 436210176 | bytes 28837476 | solution.py:130
  426.5 87.6 %all-reduce.2.cloned.1.call-done = bf16[128,8192]{1,0:T(8,128)(2,1)} async-done(((bf16[128,8192]{1,0:T(8,128)(2,1)}), bf16[128,8192]{1,0:T(8,128)(2,1)}) %all-reduce.2.cloned.1.call-update) | async-done | bytes 2097168 | tf_op jit(solution)/shard_map/psum | solution.py:139
  520.0 244.4 %while.40 = (s32[]{:T(128)}, f32[256,32,128]{2,1,0:T(8,128)}, s32[512]{0:T(512)S(1)}, bf16[512,128,128]{2,0,1:T(8,128)(2,1)}, s32[512]{0:T(512)S(1)}, /*index=5*...) while((s32[]{:T(128)}, f32[256,32,128]{2,1,0:T(8,128)}, ...), condition=%wide.region_9.10_spmd.clone, body=%wide.region_8.9_spmd.clone.sunk | while | flops 1612716032 | bytes 77596360 | solution.py:57
  532.4 8.7 %copy.76 = f32[64,128,256]{1,0,2:T(8,128)} copy(f32[64,128,256]{2,1,0:T(8,128)} %fusion.119) | data formatting | bytes 16777216 | tf_op jit(solution)/shard_map/while/body/eval_jaxpr/tsd,shd->tsh/dot_general | solution.py:31
  561.9 8.7 %copy.76 = f32[64,128,256]{1,0,2:T(8,128)} copy(f32[64,128,256]{2,1,0:T(8,128)} %fusion.119) | data formatting | bytes 16777216 | tf_op jit(solution)/shard_map/while/body/eval_jaxpr/tsd,shd->tsh/dot_general | solution.py:31
  570.6 9.8 %bitcast_add_fusion.5 = f32[256,32,128]{2,1,0:T(8,128)} fusion(f32[256,32,128]{2,1,0:T(8,128)} %get-tuple-element.546, f32[64,128,256]{1,0,2:T(8,128)} %copy.76, pred[]{:T(512)S(6)} %compare.21, s32[64]{0:T(128)S(1)} %dynamic_slice.108), kind=kOutput, calls=%fused_computation.40.clone.1 | convolution fusion | flops 807405568 | bytes 16777472 | tf_op jit(solution)/shard_map/while/body/eval_jaxpr/tsc,sj->tjc/dot_general | solution.py:33
  592.5 8.7 %copy.76 = f32[64,128,256]{1,0,2:T(8,128)} copy(f32[64,128,256]{2,1,0:T(8,128)} %fusion.119) | data formatting | bytes 16777216 | tf_op jit(solution)/shard_map/while/body/eval_jaxpr/tsd,shd->tsh/dot_general | solution.py:31
  601.3 9.8 %bitcast_add_fusion.5 = f32[256,32,128]{2,1,0:T(8,128)} fusion(f32[256,32,128]{2,1,0:T(8,128)} %get-tuple-element.546, f32[64,128,256]{1,0,2:T(8,128)} %copy.76, pred[]{:T(512)S(6)} %compare.21, s32[64]{0:T(128)S(1)} %dynamic_slice.108), kind=kOutput, calls=%fused_computation.40.clone.1 | convolution fusion | flops 807405568 | bytes 16777472 | tf_op jit(solution)/shard_map/while/body/eval_jaxpr/tsc,sj->tjc/dot_general | solution.py:33
  623.2 8.7 %copy.76 = f32[64,128,256]{1,0,2:T(8,128)} copy(f32[64,128,256]{2,1,0:T(8,128)} %fusion.119) | data formatting | bytes 16777216 | tf_op jit(solution)/shard_map/while/body/eval_jaxpr/tsd,shd->tsh/dot_general | solution.py:31
  631.9 9.8 %bitcast_add_fusion.5 = f32[256,32,128]{2,1,0:T(8,128)} fusion(f32[256,32,128]{2,1,0:T(8,128)} %get-tuple-element.546, f32[64,128,256]{1,0,2:T(8,128)} %copy.76, pred[]{:T(512)S(6)} %compare.21, s32[64]{0:T(128)S(1)} %dynamic_slice.108), kind=kOutput, calls=%fused_computation.40.clone.1 | convolution fusion | flops 807405568 | bytes 16777472 | tf_op jit(solution)/shard_map/while/body/eval_jaxpr/tsc,sj->tjc/dot_general | solution.py:33
  653.9 8.7 %copy.76 = f32[64,128,256]{1,0,2:T(8,128)} copy(f32[64,128,256]{2,1,0:T(8,128)} %fusion.119) | data formatting | bytes 16777216 | tf_op jit(solution)/shard_map/while/body/eval_jaxpr/tsd,shd->tsh/dot_general | solution.py:31
  662.6 9.8 %bitcast_add_fusion.5 = f32[256,32,128]{2,1,0:T(8,128)} fusion(f32[256,32,128]{2,1,0:T(8,128)} %get-tuple-element.546, f32[64,128,256]{1,0,2:T(8,128)} %copy.76, pred[]{:T(512)S(6)} %compare.21, s32[64]{0:T(128)S(1)} %dynamic_slice.108), kind=kOutput, calls=%fused_computation.40.clone.1 | convolution fusion | flops 807405568 | bytes 16777472 | tf_op jit(solution)/shard_map/while/body/eval_jaxpr/tsc,sj->tjc/dot_general | solution.py:33
  684.5 8.7 %copy.76 = f32[64,128,256]{1,0,2:T(8,128)} copy(f32[64,128,256]{2,1,0:T(8,128)} %fusion.119) | data formatting | bytes 16777216 | tf_op jit(solution)/shard_map/while/body/eval_jaxpr/tsd,shd->tsh/dot_general | solution.py:31
  693.3 9.8 %bitcast_add_fusion.5 = f32[256,32,128]{2,1,0:T(8,128)} fusion(f32[256,32,128]{2,1,0:T(8,128)} %get-tuple-element.546, f32[64,128,256]{1,0,2:T(8,128)} %copy.76, pred[]{:T(512)S(6)} %compare.21, s32[64]{0:T(128)S(1)} %dynamic_slice.108), kind=kOutput, calls=%fused_computation.40.clone.1 | convolution fusion | flops 807405568 | bytes 16777472 | tf_op jit(solution)/shard_map/while/body/eval_jaxpr/tsc,sj->tjc/dot_general | solution.py:33
  715.2 8.7 %copy.76 = f32[64,128,256]{1,0,2:T(8,128)} copy(f32[64,128,256]{2,1,0:T(8,128)} %fusion.119) | data formatting | bytes 16777216 | tf_op jit(solution)/shard_map/while/body/eval_jaxpr/tsd,shd->tsh/dot_general | solution.py:31
  723.9 9.8 %bitcast_add_fusion.5 = f32[256,32,128]{2,1,0:T(8,128)} fusion(f32[256,32,128]{2,1,0:T(8,128)} %get-tuple-element.546, f32[64,128,256]{1,0,2:T(8,128)} %copy.76, pred[]{:T(512)S(6)} %compare.21, s32[64]{0:T(128)S(1)} %dynamic_slice.108), kind=kOutput, calls=%fused_computation.40.clone.1 | convolution fusion | flops 807405568 | bytes 16777472 | tf_op jit(solution)/shard_map/while/body/eval_jaxpr/tsc,sj->tjc/dot_general | solution.py:33
  745.9 8.7 %copy.76 = f32[64,128,256]{1,0,2:T(8,128)} copy(f32[64,128,256]{2,1,0:T(8,128)} %fusion.119) | data formatting | bytes 16777216 | tf_op jit(solution)/shard_map/while/body/eval_jaxpr/tsd,shd->tsh/dot_general | solution.py:31
  754.6 9.8 %bitcast_add_fusion.5 = f32[256,32,128]{2,1,0:T(8,128)} fusion(f32[256,32,128]{2,1,0:T(8,128)} %get-tuple-element.546, f32[64,128,256]{1,0,2:T(8,128)} %copy.76, pred[]{:T(512)S(6)} %compare.21, s32[64]{0:T(128)S(1)} %dynamic_slice.108), kind=kOutput, calls=%fused_computation.40.clone.1 | convolution fusion | flops 807405568 | bytes 16777472 | tf_op jit(solution)/shard_map/while/body/eval_jaxpr/tsc,sj->tjc/dot_general | solution.py:33
  (227 shorter events, 444.8 us)
Async XLA Ops:
  7.2 127.7 %all-gather.5.cloned.1.call-start = ((), (), s32[]{:S(2)}) async-start(), calls=%async_computation.1 | async-start | bytes 18874368 | tf_op jit(solution)/shard_map/all_gather | solution.py:103
  42.3 241.4 %all-gather.3.cloned.1.call-start = ((), (), s32[]{:S(2)}) async-start(), calls=%async_computation | async-start | bytes 18874368 | tf_op jit(solution)/shard_map/all_gather | solution.py:104
  83.0 431.1 %all-reduce.2.cloned.1.call-start = ((), (), s32[]{:S(2)}) async-start(), calls=%async_computation.2 | async-start | bytes 4194304 | tf_op jit(solution)/shard_map/psum | solution.py:139
  135.0 2.2 copy-start.1
  154.0 2.2 copy-start.1
  172.4 2.2 copy-start.1
  190.9 2.5 copy-start.1
  209.7 2.2 copy-start.1
  228.1 2.2 copy-start.1
  246.6 2.2 copy-start.1
  265.1 2.2 copy-start.1
  520.4 2.8 copy-start
  549.9 2.8 copy-start
  580.6 2.8 copy-start
  611.2 2.8 copy-start
  641.9 2.8 copy-start
  672.6 2.8 copy-start
  703.3 2.8 copy-start
  733.9 2.8 copy-start
Sparse Core Ops, SparseCore 0:
  42.4 92.4 all-gather.4
  136.8 89.7 all-gather.2
  426.6 87.4 all-reduce.1
where the time goes:
time: 787 us; the launch traced here: 778 us
  matrix products  328 us (42%)
  local copies, waits for them, and re-layouts  294 us (37%)
  waiting for transfers between devices  135 us (17%)
  between operations  14.3 us (2%)
    dot_general x16, matrix products, spread_blocks(): jnp.einsum('tsc,sj->tjc', product, hidden_hot, precision=lax.Precision.HI...  117 us
    dot_general x16, local copies, waits for them, and re-layouts, spread_blocks(): jnp.einsum(formula, picked, weights, preferred_element_type=jnp.float32)  114 us
    dot_general x16, matrix products, spread_blocks(): jnp.einsum(formula, picked, weights, preferred_element_type=jnp.float32)  102 us
    psum x1, waiting for transfers between devices, shards(): summed = lax.psum(partial_value, 'tensor').astype(jnp.float32)  87.6 us
    all_gather x1, waiting for transfers between devices, shards(): lax.all_gather(packed_in, 'dp', axis=0, tiled=True)  47.7 us
    dot_general x8, local copies, waits for them, and re-layouts, emit_rows(): jnp.einsum('tsh,shd->tsd', picked, weights, preferred_element_type=jnp.fl...  43.2 us
    dot_general x8, matrix products, emit_rows(): jnp.einsum('tsh,shd->tsd', picked, weights, preferred_element_type=jnp.fl...  38.8 us
    dot_general x8, matrix products, emit_rows(): jnp.einsum('tsd,sq->tqd', product, place_hot, precision=lax.Precision.HIG...  34.8 us
  transfers between devices with their start and end apart: 3, of which 2 were waited for; matrix products, arithmetic and copies ran while one was open for 24% of the time, Pallas kernels for 0%

commit v1 on v0

v1 whole, which is shorter than its diff:
```python
import jax
import jax.numpy as jnp
from jax import lax
from jax.experimental import pallas as pl
from jax.experimental.pallas import tpu as pltpu
from jax.sharding import PartitionSpec as P

BLK = 128
UNROLL = 8
PIECES = 4
VMEM_CAP = 60 * 1024 * 1024


def tile_slots(strip, peer_count, capacity):
    rows, across = strip.shape
    flat = strip.reshape(peer_count, rows // peer_count * across)
    position = jnp.cumsum(flat, axis=1) - 1
    base = jnp.arange(peer_count, dtype=jnp.int32)[:, None] * capacity
    return (position + base).reshape(rows, across), position


def pair_lists(strip, slot, axis, slots):
    rows, across = strip.shape
    kept = strip.shape[1 - axis]
    pairs = -(-((slots + kept) // 2) // UNROLL) * UNROLL
    rank = jnp.cumsum(strip, axis=axis) - 1
    runs = (jnp.sum(strip, axis=axis) + 1) // 2
    start = 2 * (jnp.cumsum(runs) - runs)
    place = rank + jnp.expand_dims(start, axis)
    row = lax.broadcasted_iota(jnp.int32, strip.shape, 0)
    column = lax.broadcasted_iota(jnp.int32, strip.shape, 1)
    code = ((slot + 1) * rows + row) * across + column
    place = jnp.where(strip == 1, place, -1).reshape(1, -1)
    hit = place == jnp.arange(2 * pairs, dtype=jnp.int32)[:, None]
    found = jnp.sum(jnp.where(hit, code.reshape(1, -1), 0), axis=1)
    valid = (found > 0).astype(jnp.int32)
    source = jnp.maximum(found // (rows * across) - 1, 0)
    row_of = (found // across) % rows
    column_of = found % across
    over, along = (row_of, column_of) if axis == 0 else (column_of, row_of)
    return source, over, along[::2], valid


def pack_kernel(rows_ref, cols_ref, in_ref, out_ref, packed_in, packed_out, sems):
    count = packed_in.shape[0]

    def start(s, carry):
        r = pl.multiple_of(rows_ref[s] * BLK, BLK)
        j = pl.multiple_of(cols_ref[s] * BLK, BLK)
        pltpu.make_async_copy(
            in_ref.at[pl.ds(r, BLK), pl.ds(j, BLK)], packed_in.at[s], sems.at[0]
        ).start()
        pltpu.make_async_copy(
            out_ref.at[pl.ds(j, BLK), pl.ds(r, BLK)], packed_out.at[s], sems.at[1]
        ).start()
        return carry

    lax.fori_loop(0, count, start, 0)
    pltpu.make_async_copy(packed_in, packed_in, sems.at[0]).wait()
    pltpu.make_async_copy(packed_out, packed_out, sems.at[1]).wait()


def pack(rows, cols, weight_in, weight_out, capacity):
    shape = jax.ShapeDtypeStruct((capacity, BLK, BLK), jnp.bfloat16)
    return pl.pallas_call(
        pack_kernel,
        grid_spec=pltpu.PrefetchScalarGridSpec(
            num_scalar_prefetch=2,
            grid=(1,),
            in_specs=[pl.BlockSpec(memory_space=pl.ANY)] * 2,
            out_specs=[pl.BlockSpec((capacity, BLK, BLK), lambda i, *_: (0, 0, 0))] * 2,
            scratch_shapes=[pltpu.SemaphoreType.DMA((2,))],
        ),
        out_shape=(shape, shape),
        name="pack",
    )(rows, cols, weight_in, weight_out)


def gather_kernel(in_ref, out_ref, all_in, all_out, send, recv, local):
    me = lax.axis_index("dp")
    core, x, y = me % 2, (me // 2) % 2, me // 4

    def index(c, x_at, y_at):
        return (y_at * 2 + x_at) * 2 + c

    beside = index(core, 1 - x, y)
    above = index(core, x, 1 - y)
    across = index(core, 1 - x, 1 - y)
    partner = index(1 - core, x, y)
    barrier = pltpu.get_barrier_semaphore()
    for other in (beside, above, partner):
        pl.semaphore_signal(
            barrier, inc=1, device_id={"dp": other}, device_id_type=pl.DeviceIdType.MESH
        )
    pl.semaphore_wait(barrier, 3)

    count = in_ref.shape[0]
    pieces = PIECES if count % PIECES == 0 else 1
    size = count // pieces
    steps = range(2 * pieces)

    def own(k):
        return (in_ref, out_ref)[k // pieces].at[pl.ds((k % pieces) * size, size)]

    def held(owner, k):
        ref = (all_in, all_out)[k // pieces]
        return ref.at[pl.ds(owner * count + (k % pieces) * size, size)]

    started = []

    def move(path, k, source, owner, to):
        copy = pltpu.make_async_remote_copy(
            src_ref=source,
            dst_ref=held(owner, k),
            send_sem=send.at[path, k],
            recv_sem=recv.at[path, k],
            device_id={"dp": to},
            device_id_type=pl.DeviceIdType.MESH,
        )
        copy.start()
        started.append(copy)

    def arrive(path, k, owner, to):
        pltpu.make_async_remote_copy(
            src_ref=held(owner, k),
            dst_ref=held(owner, k),
            send_sem=send.at[path, k],
            recv_sem=recv.at[path, k],
            device_id={"dp": to},
            device_id_type=pl.DeviceIdType.MESH,
        ).wait_recv()

    for k in steps:
        move(0, k, own(k), me, beside)
        move(1, k, own(k), me, above)
        move(2, k, own(k), me, partner)
    copies = [
        pltpu.make_async_copy(own(k), held(me, k), local.at[k]) for k in steps
    ]
    for copy in copies:
        copy.start()
    for k in steps:
        arrive(0, k, beside, beside)
        if k % 2 == 0:
            move(3, k, held(beside, k), beside, above)
        move(5, k, held(beside, k), beside, partner)
        arrive(1, k, above, above)
        if k % 2 == 1:
            move(4, k, held(above, k), above, beside)
        move(6, k, held(above, k), above, partner)
    for k in steps:
        if k % 2 == 0:
            arrive(3, k, across, above)
        else:
            arrive(4, k, across, beside)
        move(7, k, held(across, k), across, partner)
    for k in steps:
        arrive(2, k, partner, partner)
        arrive(5, k, index(1 - core, 1 - x, y), partner)
        arrive(6, k, index(1 - core, x, 1 - y), partner)
        arrive(7, k, index(1 - core, 1 - x, 1 - y), partner)
    for copy in started:
        copy.wait_send()
    for copy in copies:
        copy.wait()


def gather(packed_in, packed_out, peers):
    if peers != 8:
        return (
            lax.all_gather(packed_in, "dp", axis=0, tiled=True),
            lax.all_gather(packed_out, "dp", axis=0, tiled=True),
        )
    count = packed_in.shape[0]
    shape = jax.ShapeDtypeStruct((peers * count, BLK, BLK), jnp.bfloat16)
    pieces = PIECES if count % PIECES == 0 else 1
    return pl.pallas_call(
        gather_kernel,
        out_shape=(shape, shape),
        in_specs=[pl.BlockSpec(memory_space=pltpu.VMEM)] * 2,
        out_specs=[pl.BlockSpec(memory_space=pl.ANY)] * 2,
        scratch_shapes=[
            pltpu.SemaphoreType.DMA((8, 2 * pieces)),
            pltpu.SemaphoreType.DMA((8, 2 * pieces)),
            pltpu.SemaphoreType.DMA((2 * pieces,)),
        ],
        compiler_params=pltpu.CompilerParams(collective_id=0, has_side_effects=True),
        name="gather",
    )(packed_in, packed_out)


def sweep(lists, lhs_ref, w_ref, acc, pairs, transposed):
    source, over, along, valid = lists
    acc[...] = jnp.zeros_like(acc)

    def one(p):
        parts, weights = [], []
        for k in (2 * p, 2 * p + 1):
            off = pl.multiple_of(over[k] * BLK, BLK)
            part = lhs_ref[:, pl.ds(off, BLK)]
            parts.append(jnp.where(valid[k] == 1, part, jnp.zeros_like(part)))
            weights.append(w_ref[source[k]])
        lhs = jnp.concatenate(parts, axis=1)
        if transposed:
            rhs = jnp.concatenate(weights, axis=1)
            dims = (((1,), (1,)), ((), ()))
        else:
            rhs = jnp.concatenate(weights, axis=0)
            dims = (((1,), (0,)), ((), ()))
        return along[p], lax.dot_general(lhs, rhs, dims, preferred_element_type=jnp.float32)

    def body(i, carry):
        results = [one(i * UNROLL + u) for u in range(UNROLL)]
        for place, value in results:
            acc[place] += value
        return carry

    lax.fori_loop(0, pairs // UNROLL, body, 0)


def spread(acc, out_ref, finish):
    def body(j, carry):
        at = pl.ds(pl.multiple_of(j * BLK, BLK), BLK)
        out_ref[:, at] = finish(acc[j], at)
        return carry

    lax.fori_loop(0, acc.shape[0], body, 0)


def hidden_kernel(source, over, along, valid, lhs, w, active, acc):
    sweep((source, over, along, valid), lhs, w, acc, along.shape[0], False)
    spread(acc, active, lambda a, at: jnp.tanh(a).astype(jnp.bfloat16))


def emit_kernel(source, over, along, valid, lhs, w, partial, acc):
    sweep((source, over, along, valid), lhs, w, acc, along.shape[0], False)
    spread(acc, partial, lambda a, at: a.astype(jnp.bfloat16))


def goal_kernel(source, over, along, valid, lhs, w, active, goal, acc):
    sweep((source, over, along, valid), lhs, w, acc, along.shape[0], True)
    spread(acc, goal, lambda a, at: active[:, at].astype(jnp.float32) + jnp.tanh(a))


def correct_kernel(source, over, along, valid, lhs, w, goal, result, acc):
    sweep((source, over, along, valid), lhs, w, acc, along.shape[0], True)
    spread(acc, result, lambda a, at: (goal[:, at] - jnp.tanh(a)).astype(jnp.bfloat16))


def run(kernel, name, lists, arrays, blocks, dtype):
    tok = arrays[0].shape[0]
    pairs = lists[2].shape[0]
    return pl.pallas_call(
        kernel,
        grid_spec=pltpu.PrefetchScalarGridSpec(
            num_scalar_prefetch=4,
            grid=(1,),
            in_specs=[
                pl.BlockSpec(a.shape, lambda i, *_, n=a.ndim: (0,) * n, pipeline_mode=pl.Buffered(1))
                for a in arrays
            ],
            out_specs=pl.BlockSpec((tok, blocks * BLK), lambda i, *_: (0, 0)),
            scratch_shapes=[pltpu.VMEM((blocks, tok, BLK), jnp.float32)],
        ),
        out_shape=jax.ShapeDtypeStruct((tok, blocks * BLK), dtype),
        compiler_params=pltpu.CompilerParams(vmem_limit_bytes=VMEM_CAP),
        cost_estimate=pl.CostEstimate(
            flops=pairs * 4 * tok * BLK * BLK * 4,
            bytes_accessed=sum(a.size * a.dtype.itemsize for a in arrays),
            transcendentals=0,
        ),
        name=name,
    )(*lists, *arrays)


def shards(tokens, target, weight_in, weight_out, pattern):
    peers = lax.axis_size("dp")
    data_rank = lax.axis_index("dp")
    tensor_rank = lax.axis_index("tensor")
    down = weight_in.shape[0] // BLK
    across = weight_in.shape[1] // BLK
    capacity = max(2, down * across // 4)
    slots = peers * capacity
    all_rows = tokens.shape[1] // BLK
    strip = lax.dynamic_slice_in_dim(pattern, tensor_rank * across, across, 1)
    slot, position = tile_slots(strip, peers, capacity)

    own_mask = lax.dynamic_index_in_dim(
        strip.reshape(peers, down * across), data_rank, 0, keepdims=False
    )
    own_at = lax.dynamic_index_in_dim(position, data_rank, 0, keepdims=False)
    hit = (own_at[None, :] == jnp.arange(capacity, dtype=jnp.int32)[:, None]) & (
        own_mask[None, :] == 1
    )
    within = jnp.sum(
        jnp.where(hit, jnp.arange(down * across, dtype=jnp.int32)[None, :], 0), axis=1
    )
    packed_in, packed_out = pack(
        within // across, within % across, weight_in, weight_out, capacity
    )
    gathered_in, gathered_out = gather(packed_in, packed_out, peers)

    by_hidden = pair_lists(strip, slot, 0, slots)
    by_row = pair_lists(strip, slot, 1, slots)

    active = run(
        hidden_kernel, "hidden", by_hidden, (tokens, gathered_in), across, jnp.bfloat16
    )
    partial = run(emit_kernel, "emit", by_row, (active, gathered_out), all_rows, jnp.bfloat16)
    whole_out = lax.psum(partial, "tensor")
    goal = run(
        goal_kernel, "goal", by_hidden, (target, gathered_out, active), across, jnp.float32
    )
    share = whole_out.shape[1] // lax.axis_size("tensor")
    output = lax.dynamic_slice_in_dim(whole_out, tensor_rank * share, share, 1)
    result = run(
        correct_kernel, "correct", by_hidden, (whole_out, gathered_out, goal), across, jnp.bfloat16
    )
    return output, result


def solution(mesh):
    in_specs = (P("dp", None), P("dp", None), P("dp", "tensor"), P("tensor", "dp"), P())
    out_specs = (P("dp", "tensor"), P("dp", "tensor"))
    return jax.shard_map(shards, mesh=mesh, in_specs=in_specs, out_specs=out_specs, check_vma=False)
```

time: 787 us -> 326 us (0.41); the launches traced: 778 us -> 325 us
  matrix products: 328 us -> 0 us
  local copies, waits for them, and re-layouts: 294 us -> 4.68 us
  Pallas kernels: 0 us -> 234 us
  waiting for transfers between devices: 135 us -> 65.4 us
    dot_general x74 -> x0, matrix products: 328 us -> none  [the longest x16 117 us: spread_blocks(): jnp.einsum('tsc,sj->tjc', product, hidden_hot, precision=lax.Precision.HI...]
    pallas_call x0 -> x6, Pallas kernels: none -> 234 us  [the longest x1 146 us: gather(): pl.pallas_call(gather_kernel, out_shape=(shape, shape), in_specs=[pl.Bloc...]
    dot_general x24 -> x0, local copies, waits for them, and re-layouts: 157 us -> none  [the longest x16 114 us: spread_blocks(): jnp.einsum(formula, picked, weights, preferred_element_type=jnp.float32)]
    dynamic_slice x57 -> x2, local copies, waits for them, and re-layouts: 49.7 us -> 1.89 us  [the longest x1 1.88 us: shards(): output = lax.dynamic_slice_in_dim(whole_out, tensor_rank * share, share, 1)]
    all_gather x2 -> x0, waiting for transfers between devices: 47.7 us -> none  [the longest x1 47.7 us: shards(): lax.all_gather(packed_in, 'dp', axis=0, tiled=True)]
    transpose x4 -> x0, local copies, waits for them, and re-layouts: 42.4 us -> none  [the longest x2 25.1 us: shards(): out_tile = weight_out.reshape(blocks_across, BLK, blocks_down, BLK).trans...]
    unnamed x6 -> x0, local copies, waits for them, and re-layouts: 29.6 us -> none
    psum x1, waiting for transfers between devices: 87.6 us -> 65.4 us  [shards(): whole_out = lax.psum(partial, 'tensor')]
  transfers between devices with their start and end apart: 3 -> 1, of which waited for: 2 -> 1; matrix products, arithmetic and copies ran while one was open for 24% -> 0% of each run, Pallas kernels for 0% -> 6%
where the time goes in v1:
time: 326 us; the launch traced here: 325 us
  Pallas kernels  234 us (72%)
  waiting for transfers between devices  65.4 us (20%)
  between operations  14.1 us (4%)
  other arithmetic  6.79 us (2%)
  local copies, waits for them, and re-layouts  4.68 us (1%)
    pallas_call x1, Pallas kernels, gather(): pl.pallas_call(gather_kernel, out_shape=(shape, shape), in_specs=[pl.Bloc...  146 us
    pallas_call x4, Pallas kernels, run(): pl.pallas_call(kernel, grid_spec=pltpu.PrefetchScalarGridSpec(num_scalar_...  81.3 us
    psum x1, waiting for transfers between devices, shards(): whole_out = lax.psum(partial, 'tensor')  65.4 us
  transfers between devices with their start and end apart: 1, of which 1 were waited for; matrix products, arithmetic and copies ran while one was open for 0% of the time, Pallas kernels for 6%

profile of v1, /device:TPU:0, one launch (start us, length us, event | category | flops | bytes accessed | tf_op | source)
XLA Modules:
  0.0 325.2 jit_solution(10803732310145120504)
XLA Ops:
  7.2 1.0 fusion.13
  8.3 0.6 reduce-window.27
  8.9 0.2 slice_reduce_fusion
  9.5 0.2 reduce_window_sum.55
  10.4 0.1 reduce.2
  10.7 0.1 reduce
  10.8 0.1 select_reduce_fusion.2
  10.9 0.6 and_select_fusion
  11.7 0.6 select_reduce_fusion
  12.3 0.6 compare_convert_fusion.1.valid
  12.9 0.6 add_select_fusion.6
  13.6 0.5 select_reduce_fusion.1
  14.1 0.6 compare_convert_fusion.valid
  14.7 0.6 add_select_fusion.2
  15.3 0.8 slice.14.along
  16.1 0.8 slice.15.along
  16.9 6.4 %pack.1 = (bf16[64,128,128]{2,1,0:T(8,128)(2,1)}, bf16[64,128,128]{2,1,0:T(8,128)(2,1)}) custom-call(s32[64]{0:T(128)} %get-tuple-element.22.rows_ref, s32[64]{0:T(128)} %get-tuple-element.21.cols_ref, bf16[1024,4096]{1,0:T(8,128)(2,1)} %in_ref.1, bf16[4096,1024]{1,0:T(8,128)(2,1)} %out_ref.1), custom_call_target="tpu_custom_call" | custom-call | tf_op jit(solution)/shard_map/pack/pallas_call | solution.py:65
  23.3 146.5 %gather.1 = (bf16[512,128,128]{2,1,0:T(8,128)(2,1)}, bf16[512,128,128]{2,1,0:T(8,128)(2,1)}) custom-call(bf16[64,128,128]{2,1,0:T(8,128)(2,1)} %get-tuple-element.6.in_ref, bf16[64,128,128]{2,1,0:T(8,128)(2,1)} %get-tuple-element.7.out_ref), custom_call_target="tpu_custom_call" | custom-call | tf_op jit(solution)/shard_map/gather/pallas_call | solution.py:177
  169.8 19.5 %hidden.1.lhs.active = bf16[128,4096]{1,0:T(8,128)(2,1)} custom-call(s32[544]{0:T(1024)} %get-tuple-element.17.source, s32[544]{0:T(1024)} %get-tuple-element.16.over, s32[272]{0:T(512)} %slice.15.along, s32[544]{0:T(1024)} %compare_convert_fusion.valid, bf16[128,8192]{1,0:T(8,128)(2,1)} %lhs.6, bf16[512,128,128]{2,1,0:T(8,128)(2,1)} %get-tuple-element.8.w), custom_call_target="tpu_custom_call" | custom-call | flops 9126805504 | bytes 18874368 | tf_op jit(solution)/shard_map/hidden/pallas_call | solution.py:253
  189.3 20.4 %emit.1 = bf16[128,8192]{1,0:T(8,128)(2,1)} custom-call(s32[576]{0:T(1024)} %get-tuple-element.19.source, s32[576]{0:T(1024)} %get-tuple-element.20.over, s32[288]{0:T(512)} %slice.14.along, s32[576]{0:T(1024)} %compare_convert_fusion.1.valid, bf16[128,4096]{1,0:T(8,128)(2,1)} %hidden.1.lhs.active, bf16[512,128,128]{2,1,0:T(8,128)(2,1)} %get-tuple-element.9.w), custom_call_target="tpu_custom_call" | custom-call | flops 9663676416 | bytes 17825792 | tf_op jit(solution)/shard_map/emit/pallas_call | solution.py:253
  209.7 20.8 %goal.1 = f32[128,4096]{1,0:T(8,128)} custom-call(s32[544]{0:T(1024)} %get-tuple-element.17.source, s32[544]{0:T(1024)} %get-tuple-element.16.over, s32[272]{0:T(512)} %slice.15.along, s32[544]{0:T(1024)} %compare_convert_fusion.valid, bf16[128,8192]{1,0:T(8,128)(2,1)} %lhs.7, bf16[512,128,128]{2,1,0:T(8,128)(2,1)} %get-tuple-element.9.w, ...), custom_call_target="tpu_custom_call" | custom-call | flops 9126805504 | bytes 19922944 | tf_op jit(solution)/shard_map/goal/pallas_call | solution.py:253
  230.6 65.4 %all-reduce.2.cloned.1.call-done.lhs = bf16[128,8192]{1,0:T(8,128)(2,1)} async-done(((bf16[128,8192]{1,0:T(8,128)(2,1)}), bf16[128,8192]{1,0:T(8,128)(2,1)}) %all-reduce.2.cloned.1.call-update) | async-done | bytes 2097168 | tf_op jit(solution)/shard_map/psum | solution.py:310
  296.0 1.9 constant_dynamic-slice_fusion
  297.8 20.5 %correct.1 = bf16[128,4096]{1,0:T(8,128)(2,1)} custom-call(s32[544]{0:T(1024)} %get-tuple-element.17.source, s32[544]{0:T(1024)} %get-tuple-element.16.over, s32[272]{0:T(512)} %slice.15.along, s32[544]{0:T(1024)} %compare_convert_fusion.valid, bf16[128,8192]{1,0:T(8,128)(2,1)} %all-reduce.2.cloned.1.call-done.lhs, ...), custom_call_target="tpu_custom_call" | custom-call | flops 9126805504 | bytes 20971520 | tf_op jit(solution)/shard_map/correct/pallas_call | solution.py:253
  (34 shorter events, 1.6 us)
Async XLA Ops:
  7.2 288.8 %all-reduce.2.cloned.1.call-start = ((), (), s32[]{:S(2)}) async-start(), calls=%async_computation | async-start | bytes 4194304 | tf_op jit(solution)/shard_map/psum | solution.py:310
Sparse Core Ops, SparseCore 0:
  209.8 86.0 all-reduce.1

commit v2 on v1

--- a/solution.py
+++ b/solution.py
@@ -8,6 +8,7 @@
 BLK = 128
 UNROLL = 8
 PIECES = 4
+STRIPS = 4
 VMEM_CAP = 60 * 1024 * 1024
 
 
@@ -189,6 +190,158 @@
     )(packed_in, packed_out)
 
 
+def total_kernel(n, part, total, from_left, from_right, to_right, to_left, send, recv):
+    t = lax.axis_index("tensor")
+    right, left = (t + 1) % n, (t + n - 1) % n
+    barrier = pltpu.get_barrier_semaphore()
+
+    @pl.when(t > 0)
+    def _():
+        pl.semaphore_signal(
+            barrier, inc=1, device_id={"tensor": left}, device_id_type=pl.DeviceIdType.MESH
+        )
+
+    @pl.when(t < n - 1)
+    def _():
+        pl.semaphore_signal(
+            barrier, inc=1, device_id={"tensor": right}, device_id_type=pl.DeviceIdType.MESH
+        )
+
+    inner = (t > 0) & (t < n - 1)
+
+    @pl.when(inner)
+    def _():
+        pl.semaphore_wait(barrier, 2)
+
+    @pl.when(jnp.logical_not(inner))
+    def _():
+        pl.semaphore_wait(barrier, 1)
+
+    rows, width = part.shape
+    share = width // n
+    size = rows // STRIPS
+
+    def at(ref, s, c):
+        if ref is part or ref is total:
+            return ref.at[pl.ds(c * size, size), pl.ds(s * share, share)]
+        return ref.at[s, pl.ds(c * size, size)]
+
+    def copy(path, s, c, source, landing):
+        return pltpu.make_async_remote_copy(
+            src_ref=at(source, s, c),
+            dst_ref=at(landing, s, c),
+            send_sem=send.at[path, s, c],
+            recv_sem=recv.at[path, s, c],
+            device_id={"tensor": right if path % 2 == 0 else left},
+            device_id_type=pl.DeviceIdType.MESH,
+        )
+
+    def landed(path, s, c, landing):
+        copy(path, s, c, landing, landing).wait_recv()
+
+    def add(s, c, *refs):
+        value = at(part, s, c)[...].astype(jnp.float32)
+        for ref in refs:
+            value = value + at(ref, s, c)[...].astype(jnp.float32)
+        return value.astype(part.dtype)
+
+    def inward(c):
+        for path, order, landing, stage in (
+            (0, range(n - 1, 0, -1), from_left, to_right),
+            (1, range(n - 1), from_right, to_left),
+        ):
+            first = 0 if path == 0 else n - 1
+            for s in order:
+
+                @pl.when(t == first)
+                def _():
+                    copy(path, s, c, part, landing).start()
+
+                @pl.when((t > 0) & (t < s) if path == 0 else (t < n - 1) & (t > s))
+                def _():
+                    landed(path, s, c, landing)
+                    at(stage, s, c)[...] = add(s, c, landing)
+                    copy(path, s, c, stage, landing).start()
+
+    def finish(c):
+        for s in range(n):
+
+            @pl.when(t == s)
+            def _():
+                refs = []
+                if s > 0:
+                    landed(0, s, c, from_left)
+                    refs.append(from_left)
+                if s < n - 1:
+                    landed(1, s, c, from_right)
+                    refs.append(from_right)
+                at(total, s, c)[...] = add(s, c, *refs)
+                if s < n - 1:
+                    copy(2, s, c, total, total).start()
+                if s > 0:
+                    copy(3, s, c, total, total).start()
+
+    def outward(c):
+        for distance in range(1, n):
+            for s in range(n):
+                if s + distance < n:
+
+                    @pl.when(t == s + distance)
+                    def _():
+                        landed(2, s, c, total)
+                        if s + distance < n - 1:
+                            copy(2, s, c, total, total).start()
+
+                if s - distance >= 0:
+
+                    @pl.when(t == s - distance)
+                    def _():
+                        landed(3, s, c, total)
+                        if s - distance > 0:
+                            copy(3, s, c, total, total).start()
+
+    for c in range(STRIPS + 2):
+        if c < STRIPS:
+            inward(c)
+        if 1 <= c < STRIPS + 1:
+            finish(c - 1)
+        if c >= 2:
+            outward(c - 2)
+
+    for c in range(STRIPS):
+        for s in range(n):
+            for path in range(4):
+                landing = (from_left, from_right, total, total)[path]
+                sent = (t < s, t > s, (t >= s) & (t < n - 1), (t <= s) & (t > 0))[path]
+
+                @pl.when(sent)
+                def _():
+                    copy(path, s, c, landing, landing).wait_send()
+
+
+def total_of(partial, n):
+    rows, width = partial.shape
+    if n == 1:
+        return partial
+    buffer = pltpu.VMEM((n, rows, width // n), partial.dtype)
+    return pl.pallas_call(
+        lambda *refs: total_kernel(n, *refs),
+        out_shape=jax.ShapeDtypeStruct(partial.shape, partial.dtype),
+        in_specs=[pl.BlockSpec(memory_space=pltpu.VMEM)],
+        out_specs=pl.BlockSpec(memory_space=pltpu.VMEM),
+        scratch_shapes=[
+            buffer,
+            buffer,
+            buffer,
+            buffer,
+            pltpu.SemaphoreType.DMA((4, n, STRIPS)),
+            pltpu.SemaphoreType.DMA((4, n, STRIPS)),
+        ],
+        compiler_params=pltpu.CompilerParams(collective_id=1, has_side_effects=True),
+        name="total",
+    )(partial)
+
+
 def sweep(lists, lhs_ref, w_ref, acc, pairs, transposed):
     source, over, along, valid = lists
     acc[...] = jnp.zeros_like(acc)
@@ -307,7 +460,7 @@
         hidden_kernel, "hidden", by_hidden, (tokens, gathered_in), across, jnp.bfloat16
     )
     partial = run(emit_kernel, "emit", by_row, (active, gathered_out), all_rows, jnp.bfloat16)
-    whole_out = lax.psum(partial, "tensor")
+    whole_out = total_of(partial, lax.axis_size("tensor"))
     goal = run(
         goal_kernel, "goal", by_hidden, (target, gathered_out, active), across, jnp.float32
     )

time: 326 us -> 334 us (1.025)
  Pallas kernels: 234 us -> 321 us
  waiting for transfers between devices: 65.4 us -> 0 us
  between operations: 14.1 us -> 0.74 us
    pallas_call x0 -> x1, Pallas kernels: none -> 89.1 us  [total_of(): pl.pallas_call(lambda *refs: total_kernel(n, *refs), out_shape=jax.ShapeD...]
    psum x1 -> x0, waiting for transfers between devices: 65.4 us -> none  [shards(): whole_out = lax.psum(partial, 'tensor')]
  transfers between devices with their start and end apart: 1 -> 0, of which waited for: 1 -> 0; matrix products, arithmetic and copies ran while one was open for 0% -> 0% of each run, Pallas kernels for 6% -> 0%
where the time goes in v2:
time: 334 us
  Pallas kernels  321 us (96%)
  other arithmetic  6.8 us (2%)
  local copies, waits for them, and re-layouts  4.68 us (1%)
    pallas_call x1, Pallas kernels, gather(): pl.pallas_call(gather_kernel, out_shape=(shape, shape), in_specs=[pl.Bloc...  146 us
    pallas_call x1, Pallas kernels, total_of(): pl.pallas_call(lambda *refs: total_kernel(n, *refs), out_shape=jax.ShapeD...  89.1 us
    pallas_call x4, Pallas kernels, run(): pl.pallas_call(kernel, grid_spec=pltpu.PrefetchScalarGridSpec(num_scalar_...  81.4 us

profile of v2, /device:TPU:0, one launch (start us, length us, event | category | flops | bytes accessed | tf_op | source)
XLA Modules:
  0.0 333.7 jit_solution(7149704403057549078)
XLA Ops:
  1.1 1.0 fusion.13
  2.2 0.6 reduce-window.27
  2.8 0.2 slice_reduce_fusion
  3.3 0.1 select_reduce_fusion.2
  3.6 0.1 reduce.2
  3.9 0.1 reduce
  4.0 0.6 and_select_fusion
  4.8 0.2 reduce_window_sum.55
  5.1 0.6 select_reduce_fusion
  5.8 0.5 select_reduce_fusion.1
  6.3 0.6 compare_convert_fusion.valid
  6.9 0.6 compare_convert_fusion.1.valid
  7.5 0.6 add_select_fusion.6
  8.1 0.8 slice.14.along
  8.9 0.6 add_select_fusion.2
  9.5 0.8 slice.15.along
  10.3 5.1 %pack.1 = (bf16[64,128,128]{2,1,0:T(8,128)(2,1)}, bf16[64,128,128]{2,1,0:T(8,128)(2,1)}) custom-call(s32[64]{0:T(128)} %get-tuple-element.22.rows_ref, s32[64]{0:T(128)} %get-tuple-element.21.cols_ref, bf16[1024,4096]{1,0:T(8,128)(2,1)} %in_ref.1, bf16[4096,1024]{1,0:T(8,128)(2,1)} %out_ref.1), custom_call_target="tpu_custom_call" | custom-call | tf_op jit(solution)/shard_map/pack/pallas_call | solution.py:66
  15.4 145.9 %gather.1 = (bf16[512,128,128]{2,1,0:T(8,128)(2,1)}, bf16[512,128,128]{2,1,0:T(8,128)(2,1)}) custom-call(bf16[64,128,128]{2,1,0:T(8,128)(2,1)} %get-tuple-element.6.in_ref, bf16[64,128,128]{2,1,0:T(8,128)(2,1)} %get-tuple-element.7.out_ref), custom_call_target="tpu_custom_call" | custom-call | tf_op jit(solution)/shard_map/gather/pallas_call | solution.py:178
  161.3 19.7 %hidden.1.lhs.active = bf16[128,4096]{1,0:T(8,128)(2,1)} custom-call(s32[544]{0:T(1024)} %get-tuple-element.17.source, s32[544]{0:T(1024)} %get-tuple-element.16.over, s32[272]{0:T(512)} %slice.15.along, s32[544]{0:T(1024)} %compare_convert_fusion.valid, bf16[128,8192]{1,0:T(8,128)(2,1)} %lhs.6, bf16[512,128,128]{2,1,0:T(8,128)(2,1)} %get-tuple-element.8.w), custom_call_target="tpu_custom_call" | custom-call | flops 9126805504 | bytes 18874368 | tf_op jit(solution)/shard_map/hidden/pallas_call | solution.py:406
  181.0 20.5 %emit.1.refs_0_ = bf16[128,8192]{1,0:T(8,128)(2,1)} custom-call(s32[576]{0:T(1024)} %get-tuple-element.19.source, s32[576]{0:T(1024)} %get-tuple-element.20.over, s32[288]{0:T(512)} %slice.14.along, s32[576]{0:T(1024)} %compare_convert_fusion.1.valid, bf16[128,4096]{1,0:T(8,128)(2,1)} %hidden.1.lhs.active, bf16[512,128,128]{2,1,0:T(8,128)(2,1)} %get-tuple-element.9.w), custom_call_target="tpu_custom_call" | custom-call | flops 9663676416 | bytes 17825792 | tf_op jit(solution)/shard_map/emit/pallas_call | solution.py:406
  201.5 89.1 %total.1.lhs = bf16[128,8192]{1,0:T(8,128)(2,1)} custom-call(bf16[128,8192]{1,0:T(8,128)(2,1)} %emit.1.refs_0_), custom_call_target="tpu_custom_call" | custom-call | tf_op jit(solution)/shard_map/total/pallas_call | solution.py:327
  290.7 1.9 constant_dynamic-slice_fusion
  292.5 20.6 %goal.1 = f32[128,4096]{1,0:T(8,128)} custom-call(s32[544]{0:T(1024)} %get-tuple-element.17.source, s32[544]{0:T(1024)} %get-tuple-element.16.over, s32[272]{0:T(512)} %slice.15.along, s32[544]{0:T(1024)} %compare_convert_fusion.valid, bf16[128,8192]{1,0:T(8,128)(2,1)} %lhs.7, bf16[512,128,128]{2,1,0:T(8,128)(2,1)} %get-tuple-element.9.w, ...), custom_call_target="tpu_custom_call" | custom-call | flops 9126805504 | bytes 19922944 | tf_op jit(solution)/shard_map/goal/pallas_call | solution.py:406
  313.1 20.6 %correct.1 = bf16[128,4096]{1,0:T(8,128)(2,1)} custom-call(s32[544]{0:T(1024)} %get-tuple-element.17.source, s32[544]{0:T(1024)} %get-tuple-element.16.over, s32[272]{0:T(512)} %slice.15.along, s32[544]{0:T(1024)} %compare_convert_fusion.valid, bf16[128,8192]{1,0:T(8,128)(2,1)} %total.1.lhs, bf16[512,128,128]{2,1,0:T(8,128)(2,1)} %get-tuple-element.9.w, ...), custom_call_target="tpu_custom_call" | custom-call | flops 9126805504 | bytes 20971520 | tf_op jit(solution)/shard_map/correct/pallas_call | solution.py:406
  (32 shorter events, 1.6 us)

commit v3 on v1

--- a/solution.py
+++ b/solution.py
@@ -6,8 +6,8 @@
 from jax.sharding import PartitionSpec as P
 
 BLK = 128
-UNROLL = 8
-PIECES = 4
+UNROLL = 16
+PIECES = 8
 VMEM_CAP = 60 * 1024 * 1024
 
 

time: 326 us -> 320 us (0.982)
  Pallas kernels: 234 us -> 226 us
    pallas_call x4, Pallas kernels: 81.3 us -> 71.3 us  [run(): pl.pallas_call(kernel, grid_spec=pltpu.PrefetchScalarGridSpec(num_scalar_...]
where the time goes in v3:
time: 320 us; the launch traced here: 319 us
  Pallas kernels  226 us (71%)
  waiting for transfers between devices  67.3 us (21%)
  between operations  14.1 us (4%)
  other arithmetic  6.79 us (2%)
  local copies, waits for them, and re-layouts  4.68 us (1%)
    pallas_call x1, Pallas kernels, gather(): pl.pallas_call(gather_kernel, out_shape=(shape, shape), in_specs=[pl.Bloc...  146 us
    pallas_call x4, Pallas kernels, run(): pl.pallas_call(kernel, grid_spec=pltpu.PrefetchScalarGridSpec(num_scalar_...  71.3 us
    psum x1, waiting for transfers between devices, shards(): whole_out = lax.psum(partial, 'tensor')  67.3 us
    pallas_call x1, Pallas kernels, pack(): pl.pallas_call(pack_kernel, grid_spec=pltpu.PrefetchScalarGridSpec(num_sc...  8.66 us
  transfers between devices with their start and end apart: 1, of which 1 were waited for; matrix products, arithmetic and copies ran while one was open for 0% of the time, Pallas kernels for 6%

profile of v3, /device:TPU:0, one launch (start us, length us, event | category | flops | bytes accessed | tf_op | source)
XLA Modules:
  0.0 319.4 jit_solution(5486521110690779944)
XLA Ops:
  7.2 1.0 fusion.13
  8.3 0.6 reduce-window.27
  8.9 0.2 slice_reduce_fusion
  9.5 0.2 reduce_window_sum.55
  10.4 0.1 reduce.2
  10.7 0.1 reduce
  10.8 0.1 select_reduce_fusion.2
  10.9 0.6 and_select_fusion
  11.7 0.6 select_reduce_fusion
  12.3 0.6 compare_convert_fusion.1.valid
  12.9 0.6 add_select_fusion.6
  13.6 0.5 select_reduce_fusion.1
  14.1 0.6 compare_convert_fusion.valid
  14.7 0.6 add_select_fusion.2
  15.3 0.8 slice.14.along
  16.1 0.8 slice.15.along
  16.9 8.7 %pack.1 = (bf16[64,128,128]{2,1,0:T(8,128)(2,1)}, bf16[64,128,128]{2,1,0:T(8,128)(2,1)}) custom-call(s32[64]{0:T(128)} %get-tuple-element.22.rows_ref, s32[64]{0:T(128)} %get-tuple-element.21.cols_ref, bf16[1024,4096]{1,0:T(8,128)(2,1)} %in_ref.1, bf16[4096,1024]{1,0:T(8,128)(2,1)} %out_ref.1), custom_call_target="tpu_custom_call" | custom-call | tf_op jit(solution)/shard_map/pack/pallas_call | solution.py:65
  25.6 146.5 %gather.1 = (bf16[512,128,128]{2,1,0:T(8,128)(2,1)}, bf16[512,128,128]{2,1,0:T(8,128)(2,1)}) custom-call(bf16[64,128,128]{2,1,0:T(8,128)(2,1)} %get-tuple-element.6.in_ref, bf16[64,128,128]{2,1,0:T(8,128)(2,1)} %get-tuple-element.7.out_ref), custom_call_target="tpu_custom_call" | custom-call | tf_op jit(solution)/shard_map/gather/pallas_call | solution.py:177
  172.1 17.3 %hidden.1.lhs.active = bf16[128,4096]{1,0:T(8,128)(2,1)} custom-call(s32[544]{0:T(1024)} %get-tuple-element.17.source, s32[544]{0:T(1024)} %get-tuple-element.16.over, s32[272]{0:T(512)} %slice.15.along, s32[544]{0:T(1024)} %compare_convert_fusion.valid, bf16[128,8192]{1,0:T(8,128)(2,1)} %lhs.6, bf16[512,128,128]{2,1,0:T(8,128)(2,1)} %get-tuple-element.8.w), custom_call_target="tpu_custom_call" | custom-call | flops 9126805504 | bytes 18874368 | tf_op jit(solution)/shard_map/hidden/pallas_call | solution.py:253
  189.3 18.0 %emit.1 = bf16[128,8192]{1,0:T(8,128)(2,1)} custom-call(s32[576]{0:T(1024)} %get-tuple-element.19.source, s32[576]{0:T(1024)} %get-tuple-element.20.over, s32[288]{0:T(512)} %slice.14.along, s32[576]{0:T(1024)} %compare_convert_fusion.1.valid, bf16[128,4096]{1,0:T(8,128)(2,1)} %hidden.1.lhs.active, bf16[512,128,128]{2,1,0:T(8,128)(2,1)} %get-tuple-element.9.w), custom_call_target="tpu_custom_call" | custom-call | flops 9663676416 | bytes 17825792 | tf_op jit(solution)/shard_map/emit/pallas_call | solution.py:253
  207.3 18.2 %goal.1 = f32[128,4096]{1,0:T(8,128)} custom-call(s32[544]{0:T(1024)} %get-tuple-element.17.source, s32[544]{0:T(1024)} %get-tuple-element.16.over, s32[272]{0:T(512)} %slice.15.along, s32[544]{0:T(1024)} %compare_convert_fusion.valid, bf16[128,8192]{1,0:T(8,128)(2,1)} %lhs.7, bf16[512,128,128]{2,1,0:T(8,128)(2,1)} %get-tuple-element.9.w, ...), custom_call_target="tpu_custom_call" | custom-call | flops 9126805504 | bytes 19922944 | tf_op jit(solution)/shard_map/goal/pallas_call | solution.py:253
  225.5 67.3 %all-reduce.2.cloned.1.call-done.lhs = bf16[128,8192]{1,0:T(8,128)(2,1)} async-done(((bf16[128,8192]{1,0:T(8,128)(2,1)}), bf16[128,8192]{1,0:T(8,128)(2,1)}) %all-reduce.2.cloned.1.call-update) | async-done | bytes 2097168 | tf_op jit(solution)/shard_map/psum | solution.py:310
  292.8 1.9 constant_dynamic-slice_fusion
  294.7 17.8 %correct.1 = bf16[128,4096]{1,0:T(8,128)(2,1)} custom-call(s32[544]{0:T(1024)} %get-tuple-element.17.source, s32[544]{0:T(1024)} %get-tuple-element.16.over, s32[272]{0:T(512)} %slice.15.along, s32[544]{0:T(1024)} %compare_convert_fusion.valid, bf16[128,8192]{1,0:T(8,128)(2,1)} %all-reduce.2.cloned.1.call-done.lhs, ...), custom_call_target="tpu_custom_call" | custom-call | flops 9126805504 | bytes 20971520 | tf_op jit(solution)/shard_map/correct/pallas_call | solution.py:253
  (34 shorter events, 1.6 us)
Async XLA Ops:
  7.2 285.7 %all-reduce.2.cloned.1.call-start = ((), (), s32[]{:S(2)}) async-start(), calls=%async_computation | async-start | bytes 4194304 | tf_op jit(solution)/shard_map/psum | solution.py:310
Sparse Core Ops, SparseCore 0:
  207.5 85.3 all-reduce.1
